TPU v7x, 128 devices: a whole 4x4x4 slice. The times are simulated.
128 devices in a mesh: obs: 4 (over z_hi, core), par: 32 (over y, x, z_lo).
Axes of the slice: x: 4, y: 4, z: 4 (z_hi: 2, z_lo: 2; z = z_hi * 2 + z_lo), core: 2. Of those that a mesh axis runs over, the one named last changes fastest.
Arguments:
- jacobian: bfloat16 [3072, 16384], P(('obs', 'par')), may hold values from -0.109375 to 0.109375
- obs_weights: float32 [3072], replicated, may hold values from 0.1 to 10
- time_to_obs: int32 [3072], P(('obs', 'par')), may hold values from 0 to 3071, each once
Outputs:
- normal_matrix: float32 [16384, 16384], P('obs', 'par')
Inputs may be any that keep to these rules, and one draw needn't show every extreme that they name: `time_to_obs`: each observation index appears exactly once.
All inputs are finite; a program needn't handle non-finite values.
Results may differ from a plain program's by a relative error of at most 0.0039.
Values may be sent and summed in bfloat16 or wider, within the bound.
No kernel may reach another device: no remote copies, remote signals or barrier semaphores. Data moves between devices by JAX's collectives and lax.ppermute only.
A program may use at most 128 MiB of HBM per device.

v0:
```python
import jax
import jax.numpy as jnp
from jax import lax
from jax.sharding import PartitionSpec as P


def on_device(jacobian, obs_weights, time_to_obs):
    rows_here = jacobian.shape[0]
    param_count = jacobian.shape[1]
    obs_count = lax.axis_size("obs")
    par_count = lax.axis_size("par")
    indices = jnp.arange(obs_weights.shape[0], dtype=jnp.int32)
    picked = jnp.sum(
        jnp.where(time_to_obs[:, None] == indices[None, :], obs_weights[None, :], 0.0), axis=1
    )
    scaled = (jnp.sqrt(picked)[:, None] * jacobian.astype(jnp.float32)).astype(jnp.bfloat16)
    lifted = scaled.reshape(1, rows_here, param_count)
    blocks = lax.all_to_all(lifted, "obs", split_axis=2, concat_axis=0, tiled=True)
    col_width = param_count // par_count
    columns = lax.all_to_all(lifted, "par", split_axis=2, concat_axis=0, tiled=True)
    columns = lax.all_gather(columns, "obs", axis=0, tiled=True)
    columns = columns.reshape(obs_count, par_count * rows_here, col_width)
    panels = lax.all_gather(blocks, "par", axis=1, tiled=True)
    return jnp.einsum("arc,ard->cd", panels, columns, preferred_element_type=jnp.float32)


def solution(mesh):
    placed = (P(("obs", "par"), None), P(), P(("obs", "par")))
    return jax.shard_map(
        on_device, mesh=mesh, in_specs=placed, out_specs=P("obs", "par"), check_vma=False
    )
```

profile of v0, /device:TPU:34, one launch (start us, length us, event | category | flops | bytes accessed | tf_op | source)
XLA Modules:
  0.0 776.7 jit_solution(6125067894253872118)
XLA Ops:
  6.5 0.0 all-gather.5.cloned.1.call-start
  6.5 0.9 select_reduce_fusion
  7.5 1.3 fusion.5
  8.8 12.5 %copy.17 = bf16[1,24,16384]{1,0,2:T(2,128)(2,1)} copy(bf16[1,24,16384]{2,1,0:T(8,128)(2,1)S(1)} %fusion.5) | data formatting | bytes 1572864 | tf_op jit(solution)/shard_map/reshape | solution.py:17
  21.3 0.5 broadcast.2
  21.8 90.6 %reduce.1 = bf16[16384,24]{1,0:T(8,128)(2,1)} reduce(bf16[16384,1,24]{2,1,0:T(2,128)(2,1)} %bitcast.26, bf16[]{:T(256)} %broadcast.2), dimensions={1}, to_apply=%bitcast.22.reduce_sub_computation | reduce | bytes 1572866
  112.5 6.6 reshape.19
  119.1 17.2 %all_to_all.36 = bf16[4,2,49152]{2,1,0:T(2,128)(2,1)S(1)} all-to-all(bf16[4,2,49152]{2,1,0:T(2,128)(2,1)S(1)} %reshape.19), channel_id=1, replica_groups=mesh['obs'=4,'par'=32] {'obs'}, dimensions={0} | all-to-all | bytes 1572864 | tf_op jit(solution)/shard_map/all_to_all | solution.py:18
  136.3 12.0 %reshape.20 = bf16[16384,1,24]{2,1,0:T(2,128)(2,1)} reshape(bf16[4,2,49152]{2,1,0:T(2,128)(2,1)S(1)} %all_to_all.36) | data formatting | bytes 1572864
  148.3 15.2 %copy.18 = bf16[1,24,16384]{2,1,0:T(8,128)(2,1)S(1)} copy(bf16[1,24,16384]{1,0,2:T(2,128)(2,1)} %bitcast.28) | data formatting | bytes 1572864 | tf_op jit(solution)/shard_map/all_to_all | solution.py:18
  163.5 1.5 all_to_all.27
  165.0 0.0 all-gather.5.cloned.1.call-update
  165.0 0.2 all-gather.7.cloned.1.call-start
  165.2 90.7 %reduce = bf16[16384,24]{1,0:T(8,128)(2,1)} reduce(bf16[16384,1,24]{2,1,0:T(2,128)(2,1)} %bitcast.27, bf16[]{:T(256)} %broadcast.2), dimensions={1}, to_apply=%bitcast.20.reduce_sub_computation | reduce | bytes 1572866
  255.9 7.4 reshape.17
  263.3 23.5 %all_to_all.37 = bf16[32,2,6144]{2,1,0:T(2,128)(2,1)S(1)} all-to-all(bf16[32,2,6144]{2,1,0:T(2,128)(2,1)S(1)} %reshape.17), channel_id=1, replica_groups=mesh['obs'=4,'par'=32] {'par'}, dimensions={0} | all-to-all | bytes 1572864 | tf_op jit(solution)/shard_map/all_to_all | solution.py:20
  286.8 17.3 %reshape.18 = bf16[16384,1,24]{2,1,0:T(2,128)(2,1)} reshape(bf16[32,2,6144]{2,1,0:T(2,128)(2,1)S(1)} %all_to_all.37) | data formatting | bytes 1572864
  304.1 15.2 %copy.22 = bf16[1,24,16384]{2,1,0:T(8,128)(2,1)S(1)} copy(bf16[1,24,16384]{1,0,2:T(2,128)(2,1)} %bitcast.29) | data formatting | bytes 1572864 | tf_op jit(solution)/shard_map/all_to_all | solution.py:20
  319.3 0.2 copy.24
  319.6 0.1 bitcast_bitcast_fusion
  319.6 1.3 copy.23
  320.9 0.0 all-gather.7.cloned.1.call-update
  321.0 388.9 %all-gather.5.cloned.1.call-done = bf16[4,1,768,4096]{3,0,1,2:T(4,128)(2,1)} async-done(((bf16[4,1,24,4096]{3,0,1,2:T(4,128)(2,1)}), bf16[4,1,768,4096]{3,0,1,2:T(4,128)(2,1)}) %all-gather.5.cloned.1.call-update) | async-done | bytes 25165840 | tf_op jit(solution)/shard_map/all_gather | solution.py:23
  709.9 39.0 %copy.20 = bf16[4,1,768,4096]{2,3,0,1:T(8,128)(2,1)} copy(bf16[4,1,768,4096]{3,0,1,2:T(4,128)(2,1)} %all-gather.5.cloned.1.call-done) | data formatting | bytes 50331648 | tf_op jit(solution)/shard_map/all_gather | solution.py:23
  748.9 0.0 all-gather.7.cloned.1.call-done
  748.9 20.9 %fusion.2 = f32[4096,512]{1,0:T(8,128)} fusion(bf16[4,768,512]{2,1,0:T(8,128)(2,1)} %bitcast.33, bf16[4,1,768,4096]{2,3,0,1:T(8,128)(2,1)} %copy.20), kind=kOutput, calls=%fused_computation.2 | convolution fusion | flops 12884901888 | bytes 36700160 | tf_op jit(solution)/shard_map/arc,ard->cd/dot_general | solution.py:24
  (1 shorter events, 0.0 us)
Async XLA Ops:
  6.5 703.4 %all-gather.5.cloned.1.call-start = ((), (), s32[]{:S(2)}) async-start(), calls=%async_computation.2 | async-start | bytes 25952256 | tf_op jit(solution)/shard_map/all_gather | solution.py:23
  165.0 583.9 %all-gather.7.cloned.1.call-start = ((), (), s32[]{:S(2)}) async-start(), calls=%async_computation.3 | async-start | bytes 3932160 | tf_op jit(solution)/shard_map/all_gather | solution.py:21
Sparse Core Ops, SparseCore 0:
  165.1 544.7 all-gather.4
  711.6 31.3 all-gather.6
where the time goes:
time: 779 us; the launch traced here: 777 us
  waiting for transfers between devices  389 us (50%)
  other arithmetic  184 us (24%)
  local copies, waits for them, and re-layouts  129 us (17%)
  blocking collectives  40.7 us (5%)
  matrix products  20.9 us (3%)
  between operations  13.5 us (2%)
    all_gather x1, waiting for transfers between devices, on_device(): panels = lax.all_gather(blocks, 'par', axis=1, tiled=True)  389 us
    unnamed x2, other arithmetic  181 us
    unnamed x6, local copies, waits for them, and re-layouts  44.1 us
    all_gather x1, local copies, waits for them, and re-layouts, on_device(): panels = lax.all_gather(blocks, 'par', axis=1, tiled=True)  39 us
    all_to_all x1, blocking collectives, on_device(): lax.all_to_all(lifted, 'par', split_axis=2, concat_axis=0, tiled=True)  23.5 us
    dot_general x1, matrix products, on_device(): jnp.einsum('arc,ard->cd', panels, columns, preferred_element_type=jnp.flo...  20.9 us
    all_to_all x1, blocking collectives, on_device(): lax.all_to_all(lifted, 'obs', split_axis=2, concat_axis=0, tiled=True)  17.2 us
    all_to_all x2, local copies, waits for them, and re-layouts, on_device(): lax.all_to_all(lifted, 'obs', split_axis=2, concat_axis=0, tiled=True)  16.7 us
  transfers between devices with their start and end apart: 2, of which 1 were waited for; matrix products, arithmetic and copies ran while one was open for 22% of the time, Pallas kernels for 0%

commit v1 on v0

--- a/solution.py
+++ b/solution.py
@@ -15,7 +15,10 @@
     )
     scaled = (jnp.sqrt(picked)[:, None] * jacobian.astype(jnp.float32)).astype(jnp.bfloat16)
     lifted = scaled.reshape(1, rows_here, param_count)
-    blocks = lax.all_to_all(lifted, "obs", split_axis=2, concat_axis=0, tiled=True)
+    blocks = jnp.concatenate(
+        lax.all_to_all(jnp.stack(jnp.split(lifted, lax.axis_size("obs"), axis=2)), "obs", 0, 0),
+        axis=0,
+    )
     col_width = param_count // par_count
     columns = lax.all_to_all(lifted, "par", split_axis=2, concat_axis=0, tiled=True)
     columns = lax.all_gather(columns, "obs", axis=0, tiled=True)

time: 779 us -> 641 us (0.82)
  other arithmetic: 184 us -> 93.1 us
  local copies, waits for them, and re-layouts: 129 us -> 95.1 us
  waiting for transfers between devices: 389 us -> 376 us
    unnamed x2 -> x1, other arithmetic: 181 us -> 90.7 us
    unnamed x6 -> x4, local copies, waits for them, and re-layouts: 44.1 us -> 25.5 us
    all_to_all x2 -> x1, local copies, waits for them, and re-layouts: 16.7 us -> 1.53 us  [on_device(): lax.all_to_all(jnp.stack(jnp.split(lifted, lax.axis_size('obs'), axis=2))...]
    all_gather x1, waiting for transfers between devices: 389 us -> 376 us  [on_device(): panels = lax.all_gather(blocks, 'par', axis=1, tiled=True)]
  transfers between devices with their start and end apart: 2 -> 2, of which waited for: 1 -> 1; matrix products, arithmetic and copies ran while one was open for 22% -> 29% of each run, Pallas kernels for 0% -> 0%
where the time goes in v1:
time: 641 us; the launch traced here: 639 us
  waiting for transfers between devices  376 us (59%)
  local copies, waits for them, and re-layouts  95.1 us (15%)
  other arithmetic  93.1 us (15%)
  blocking collectives  41 us (6%)
  matrix products  20.9 us (3%)
  between operations  13.5 us (2%)
    all_gather x1, waiting for transfers between devices, on_device(): panels = lax.all_gather(blocks, 'par', axis=1, tiled=True)  376 us
    unnamed x1, other arithmetic  90.7 us
    all_gather x1, local copies, waits for them, and re-layouts, on_device(): panels = lax.all_gather(blocks, 'par', axis=1, tiled=True)  38.9 us
    unnamed x4, local copies, waits for them, and re-layouts  25.5 us
    all_to_all x1, blocking collectives, on_device(): lax.all_to_all(lifted, 'par', split_axis=2, concat_axis=0, tiled=True)  23.8 us
    dot_general x1, matrix products, on_device(): jnp.einsum('arc,ard->cd', panels, columns, preferred_element_type=jnp.flo...  20.9 us
    all_to_all x1, blocking collectives, on_device(): lax.all_to_all(jnp.stack(jnp.split(lifted, lax.axis_size('obs'), axis=2))...  17.2 us
    all_to_all x3, local copies, waits for them, and re-layouts, on_device(): lax.all_to_all(lifted, 'par', split_axis=2, concat_axis=0, tiled=True)  16.6 us
  transfers between devices with their start and end apart: 2, of which 1 were waited for; matrix products, arithmetic and copies ran while one was open for 29% of the time, Pallas kernels for 0%

profile of v1, /device:TPU:34, one launch (start us, length us, event | category | flops | bytes accessed | tf_op | source)
XLA Modules:
  0.0 639.3 jit_solution(7465687384219261055)
XLA Ops:
  6.5 0.0 all-gather.5.cloned.1.call-start
  6.5 0.9 select_reduce_fusion
  7.5 1.3 fusion.5
  8.8 0.1 slice_bitcast_fusion.3
  8.9 0.1 pad_maximum_fusion
  9.0 17.2 %all_to_all.23 = bf16[4,1,24,4096]{3,2,1,0:T(8,128)(2,1)S(1)} all-to-all(bf16[4,1,24,4096]{3,2,1,0:T(8,128)(2,1)S(1)} %pad_maximum_fusion), channel_id=1, replica_groups=mesh['obs'=4,'par'=32] {'obs'}, dimensions={0} | all-to-all | bytes 1572864 | tf_op jit(solution)/shard_map/all_to_all | solution.py:19
  26.2 1.5 copy.22
  27.7 0.0 all-gather.5.cloned.1.call-update
  27.7 0.0 all-gather.7.cloned.1.call-start
  27.8 12.5 %copy.24 = bf16[1,24,16384]{1,0,2:T(2,128)(2,1)} copy(bf16[1,24,16384]{2,1,0:T(8,128)(2,1)S(1)} %fusion.5) | data formatting | bytes 1572864 | tf_op jit(solution)/shard_map/reshape | solution.py:17
  40.3 0.6 broadcast.2
  40.9 90.7 %reduce = bf16[16384,24]{1,0:T(8,128)(2,1)} reduce(bf16[16384,1,24]{2,1,0:T(2,128)(2,1)} %bitcast.29, bf16[]{:T(256)} %broadcast.2), dimensions={1}, to_apply=%bitcast.25.reduce_sub_computation | reduce | bytes 1572866
  131.6 7.4 %reshape.21 = bf16[32,2,6144]{2,1,0:T(2,128)(2,1)S(1)} reshape(bf16[16384,24]{1,0:T(8,128)(2,1)} %reduce) | data formatting | bytes 1572864
  139.0 23.8 %all_to_all.24 = bf16[32,2,6144]{2,1,0:T(2,128)(2,1)S(1)} all-to-all(bf16[32,2,6144]{2,1,0:T(2,128)(2,1)S(1)} %reshape.21), channel_id=1, replica_groups=mesh['obs'=4,'par'=32] {'par'}, dimensions={0} | all-to-all | bytes 1572864 | tf_op jit(solution)/shard_map/all_to_all | solution.py:23
  162.8 17.3 %reshape.22 = bf16[16384,1,24]{2,1,0:T(2,128)(2,1)} reshape(bf16[32,2,6144]{2,1,0:T(2,128)(2,1)S(1)} %all_to_all.24) | data formatting | bytes 1572864
  180.2 15.2 %copy.25 = bf16[1,24,16384]{2,1,0:T(8,128)(2,1)S(1)} copy(bf16[1,24,16384]{1,0,2:T(2,128)(2,1)} %bitcast.30) | data formatting | bytes 1572864 | tf_op jit(solution)/shard_map/all_to_all | solution.py:23
  195.4 0.2 copy.27
  195.6 0.1 bitcast_bitcast_fusion
  195.7 1.3 copy.26
  197.0 0.0 all-gather.7.cloned.1.call-update
  197.0 375.6 %all-gather.5.cloned.1.call-done = bf16[4,1,768,4096]{3,0,1,2:T(4,128)(2,1)} async-done(((bf16[4,1,24,4096]{3,0,1,2:T(4,128)(2,1)}), bf16[4,1,768,4096]{3,0,1,2:T(4,128)(2,1)}) %all-gather.5.cloned.1.call-update) | async-done | bytes 25165840 | tf_op jit(solution)/shard_map/all_gather | solution.py:26
  572.7 38.9 %copy.23 = bf16[4,1,768,4096]{2,3,0,1:T(8,128)(2,1)} copy(bf16[4,1,768,4096]{3,0,1,2:T(4,128)(2,1)} %all-gather.5.cloned.1.call-done) | data formatting | bytes 50331648 | tf_op jit(solution)/shard_map/all_gather | solution.py:26
  611.6 0.0 all-gather.7.cloned.1.call-done
  611.6 20.9 %fusion.2 = f32[4096,512]{1,0:T(8,128)} fusion(bf16[4,768,512]{2,1,0:T(8,128)(2,1)} %bitcast.33, bf16[4,1,768,4096]{2,3,0,1:T(8,128)(2,1)} %copy.23), kind=kOutput, calls=%fused_computation.2 | convolution fusion | flops 12884901888 | bytes 36700160 | tf_op jit(solution)/shard_map/arc,ard->cd/dot_general | solution.py:27
  (1 shorter events, 0.0 us)
Async XLA Ops:
  6.5 566.1 %all-gather.5.cloned.1.call-start = ((), (), s32[]{:S(2)}) async-start(), calls=%async_computation.2 | async-start | bytes 25952256 | tf_op jit(solution)/shard_map/all_gather | solution.py:26
  27.7 583.9 %all-gather.7.cloned.1.call-start = ((), (), s32[]{:S(2)}) async-start(), calls=%async_computation.3 | async-start | bytes 3932160 | tf_op jit(solution)/shard_map/all_gather | solution.py:24
Sparse Core Ops, SparseCore 0:
  27.9 544.7 all-gather.4
  574.3 31.3 all-gather.6
